TPU v7x, 32 devices: a whole 2x2x4 slice. The times are simulated.
32 devices in a mesh: slab: 4 (over y, core), bl: 8 (over z, x).
Axes of the slice: x: 2, y: 2, z: 4, core: 2. Of those that a mesh axis runs over, the one named last changes fastest.
Arguments:
- model_image: float32 [2, 8192, 8192], P(None, 'slab', 'bl'), may hold values from -6 to 6
- vis_coords: float32 [512, 2, 128], P(('slab', 'bl')), may hold values from 0 to 32
- vis_observed: float32 [512, 2, 128], P(('slab', 'bl')), may hold values from -6 to 6
- tile_slot: int32 [512], P(('slab', 'bl')), may hold values from 0 to 2047
- tile_group: int32 [512, 1], P(('slab', 'bl')), may hold values from 0 to 7; in each aligned block of 16 rows (0 to 15, 16 to 31, ...) at most 8 rows name the same one
- w_plane: int32 [512], P(('slab', 'bl')), may hold values from 0 to 7
- vis_count: int32 [512], P(('slab', 'bl')), may hold values from 16 to 128, as said below
Outputs:
- residual_image: float32 [2, 8192, 8192], P(None, 'slab', 'bl')
- residual_vis: float32 [512, 2, 128], P(('slab', 'bl'))
Inputs may be any that keep to these rules, and one draw needn't show every extreme that they name: `tile_group`: among the 16 subgrids of one device, at most 8 name the same group. `vis_count`: some subgrid holds exactly 128 visibilities.
All inputs are finite; a program needn't handle non-finite values.
Results may differ from a plain program's by a relative error of at most 0.0003.
Values sent between devices are 32-bit elements; how exact they have to be, the bound alone decides.
No kernel may reach another device: no remote copies, remote signals or barrier semaphores. Data moves between devices by JAX's collectives and lax.ppermute only.
A program may use at most 192 MiB of HBM per device.

v0:
```python
import math
import jax
import jax.numpy as jnp
from jax import lax
from jax.sharding import PartitionSpec as P

SUB = 32
w_step = 0.1


def complex_einsum(form, left, right):
    product = lambda first, second: jnp.einsum(form, first, second, precision=lax.Precision.HIGHEST)
    return (
        product(left[0], right[0]) - product(left[1], right[1]),
        product(left[0], right[1]) + product(left[1], right[0]),
    )


def complex_mul(left, right):
    return (left[0] * right[0] - left[1] * right[1], left[0] * right[1] + left[1] * right[0])


def subgrid_pass(tile_real, tile_imag, coords, observed, planes, counts):
    width = tile_real.shape[-1]
    half = width // 2
    slots = coords.shape[-1]
    index = jnp.arange(width, dtype=jnp.int32)
    offsets = (index - half).astype(jnp.float32)
    turns = index[:, None] * (index[None, :] - half) % width
    angle = 2.0 * math.pi / width * turns.astype(jnp.float32)
    forward_d = (jnp.cos(angle), jnp.sin(angle))
    backward_d = (forward_d[0], -forward_d[1])
    scale_sub = 1.0 / (width * width)
    halfway = complex_einsum("il,kij->klj", forward_d, (tile_real, tile_imag))
    image_sub = complex_einsum("klj,jm->klm", halfway, forward_d)
    image_sub = (image_sub[0] * scale_sub, image_sub[1] * scale_sub)
    radius = (offsets[:, None] ** 2 + offsets[None, :] ** 2) / (half * half)
    phase = -w_step * planes.astype(jnp.float32)[:, None, None] * radius[None]
    screen = (jnp.cos(phase), jnp.sin(phase))
    weighted = complex_mul(screen, image_sub)
    along_a = -2.0 * math.pi / width * coords[:, 0, :][:, None, :] * offsets[None, :, None]
    along_b = -2.0 * math.pi / width * coords[:, 1, :][:, None, :] * offsets[None, :, None]
    phase_a = (jnp.cos(along_a), jnp.sin(along_a))
    phase_b = (jnp.cos(along_b), jnp.sin(along_b))
    partial_rows = complex_einsum("klm,kmj->klj", weighted, phase_b)
    terms = complex_mul(phase_a, partial_rows)
    predicted = (jnp.sum(terms[0], axis=1), jnp.sum(terms[1], axis=1))
    live = (jnp.arange(slots, dtype=jnp.int32)[None, :] < counts[:, None]).astype(jnp.float32)
    resid_real = (observed[:, 0, :] - predicted[0]) * live
    resid_imag = (observed[:, 1, :] - predicted[1]) * live
    spread = complex_mul(
        (phase_a[0], -phase_a[1]), (resid_real[:, None, :], resid_imag[:, None, :])
    )
    collected = complex_einsum("klj,kmj->klm", spread, (phase_b[0], -phase_b[1]))
    unscreened = complex_mul((screen[0], -screen[1]), collected)
    middle = complex_einsum("il,klm->kim", backward_d, unscreened)
    tile_out = complex_einsum("kim,jm->kij", middle, backward_d)
    return (
        jnp.stack([resid_real, resid_imag], axis=1),
        jnp.stack([tile_out[0] * scale_sub, tile_out[1] * scale_sub], axis=1),
    )


def table(product, modulus, sign):
    angle = 2.0 * math.pi / modulus * (product % modulus).astype(jnp.float32)
    return (jnp.cos(angle), sign * jnp.sin(angle))


def real_form(pair):
    return jnp.stack(
        [jnp.stack([pair[0], -pair[1]], axis=1), jnp.stack([pair[1], pair[0]], axis=1)], axis=0
    )


def product_high(form, left, right):
    return jnp.einsum(form, left, right, precision=lax.Precision.HIGH)


def twist(pair, values):
    return jnp.stack(complex_mul(pair, (values[0], values[1])))


def per_device(model_image, vis_coords, vis_observed, tile_slot, tile_group, w_plane, vis_count):
    groups = lax.axis_size("bl")
    bands = lax.axis_size("slab")
    both = ("slab", "bl")
    width_in = model_image.shape[2]
    extent = model_image.shape[1] * bands
    tile_rows = extent // SUB
    owned_cols = tile_rows // (groups * bands)
    sub_count = tile_slot.shape[0]
    tile_u = tile_slot % tile_rows
    tile_v = (
        lax.axis_index("slab") * groups + tile_group[:, 0]
    ) * owned_cols + tile_slot // tile_rows
    ids = lax.all_gather(tile_u * tile_rows + tile_v, both, axis=0, tiled=True)
    all_u = ids // tile_rows
    all_v = ids % tile_rows
    image = lax.all_to_all(model_image, "slab", split_axis=2, concat_axis=1, tiled=True)
    cols = image.shape[2]
    col = (
        lax.axis_index("bl") * width_in
        + lax.axis_index("slab") * cols
        + jnp.arange(cols, dtype=jnp.int32)
    )
    short = jnp.arange(SUB, dtype=jnp.int32)
    long = jnp.arange(tile_rows, dtype=jnp.int32)
    coarse = table(short[:, None] * short[None, :], SUB, -1.0)
    fine = table(short[:, None] * long[None, :], extent, -1.0)
    pick_u = table(all_u[:, None] * long[None, :], tile_rows, -1.0)
    shift_v = table(all_v[:, None] * col[None, :], tile_rows, -1.0)
    inside_v = table(short[:, None] * col[None, :], extent, -1.0)
    conj = lambda pair: (pair[0], -pair[1])
    lift_fine = lambda pair: (pair[0][:, :, None], pair[1][:, :, None])
    lift_v = lambda pair: (pair[0][:, None, :], pair[1][:, None, :])
    stage = product_high(
        "aibq,bqpc->aipc", real_form(coarse), image.reshape(2, SUB, tile_rows, cols)
    )
    stage = twist(lift_fine(fine), stage)
    strips = product_high("agbp,bipc->agic", real_form(pick_u), stage)
    strips = twist(lift_v(shift_v), strips)
    partial = product_high("ajbc,bgic->gaij", real_form(inside_v), strips) / extent
    mine = lax.psum_scatter(
        partial.reshape(-1, 2 * SUB * SUB), both, scatter_dimension=0, tiled=True
    )
    mine = mine.reshape(sub_count, 2, SUB, SUB)
    residual_vis, contrib = subgrid_pass(
        mine[:, 0], mine[:, 1], vis_coords, vis_observed, w_plane, vis_count
    )
    every = lax.all_gather(contrib.reshape(sub_count, 2 * SUB * SUB), both, axis=0, tiled=True)
    every = every.reshape(-1, 2, SUB, SUB)
    spread = product_high("ajbc,gaij->bgic", real_form(inside_v), every)
    spread = twist(lift_v(conj(shift_v)), spread)
    back = product_high("agbp,agic->bipc", real_form(pick_u), spread)
    back = twist(lift_fine(conj(fine)), back) / extent
    rows = product_high("aibq,aipc->bqpc", real_form(coarse), back)
    residual_image = lax.all_to_all(
        rows.reshape(2, extent, cols), "slab", split_axis=1, concat_axis=2, tiled=True
    )
    return (residual_image, residual_vis)


def solution(mesh):
    placed = (
        P(None, "slab", "bl"),
        P(("slab", "bl"), None, None),
        P(("slab", "bl"), None, None),
        P(("slab", "bl")),
        P(("slab", "bl"), None),
        P(("slab", "bl")),
        P(("slab", "bl")),
    )
    return jax.shard_map(
        per_device,
        mesh=mesh,
        in_specs=placed,
        out_specs=(P(None, "slab", "bl"), P(("slab", "bl"), None, None)),
        check_vma=False,
    )
```

profile of v0, /device:TPU:0, one launch (start us, length us, event | category | flops | bytes accessed | tf_op | source)
XLA Modules:
  0.0 1117.9 jit_solution(155449338450149249)
XLA Ops:
  7.2 25.3 %copy.94 = f32[2,2048,1024]{1,0,2:T(2,128)} copy(f32[2,2048,1024]{2,1,0:T(8,128)} %param.7) | data formatting | bytes 33554432 | tf_op args[0]
  32.5 7.1 all-to-all-start
  39.8 218.7 %all-reduce = s32[512]{0:T(512)S(1)} all-reduce(s32[512]{0:T(512)S(1)} %fusion.206), channel_id=1, replica_groups=mesh['slab'=4,'bl'=8] {'slab','bl'}, use_global_device_ids=true, to_apply=%add | all-reduce | flops 512 | bytes 4096
  265.5 17.7 %copy.95 = f32[2,2048,1024]{1,2,0:T(8,128)} copy(f32[2,2048,1024]{1,0,2:T(2,128)} %all-to-all-done) | data formatting | bytes 33554432 | tf_op jit(solution)/shard_map/all_to_all | solution.py:99
  283.3 16.5 %copy.96 = f32[2,4,2048,256]{3,2,1,0:T(8,128)} copy(f32[2,4,2048,256]{2,3,1,0:T(8,128)} %bitcast.175) | data formatting | bytes 33554432 | tf_op jit(solution)/shard_map/all_to_all | solution.py:99
  299.8 26.3 %fusion.15 = f32[2,32,256,256]{3,1,2,0:T(8,128)} fusion(f32[2,32,256,256]{3,2,1,0:T(8,128)} %bitcast.174, f32[1,32,2,32]{3,1,2,0:T(8,128)S(1)} %get-tuple-element.27, f32[1,32,2,32]{3,1,2,0:T(8,128)S(1)} %get-tuple-element.26), kind=kOutput, calls=%fused_computation.27 | convolution fusion | flops 1610616832 | bytes 33570816 | tf_op jit(solution)/shard_map/aibq,bqpc->aipc/dot_general | solution.py:76
  326.1 13.7 %multiply_subtract_fusion.3 = (f32[1,32,256,256]{3,1,2,0:T(8,128)}, f32[1,32,256,256]{3,1,2,0:T(8,128)}) fusion(f32[2,32,256,256]{3,1,2,0:T(8,128)} %fusion.15, f32[32,256]{0,1:T(8,128)S(1)} %copy-done.3, f32[32,256]{0,1:T(8,128)S(1)} %get-tuple-element.42), kind=kLoop, calls=%fused_computation.26 | loop fusion | flops 12582912 | bytes 33619968 | tf_op jit(solution)/shard_map/sub | solution.py:20
  346.4 42.2 %convolution_bitcast_fusion.1 = f32[2,512,32,256]{3,1,2,0:T(8,128)} fusion(f32[2,32,256,256]{3,1,2,0:T(8,128)S(1)} %pad_maximum_fusion, f32[1,512,2,256]{3,1,2,0:T(8,128)S(1)} %get-tuple-element.19, f32[1,512,2,256]{3,1,2,0:T(8,128)S(1)} %get-tuple-element.18), kind=kOutput, calls=%fused_computation.7 | convolution fusion | flops 25770328064 | bytes 52428800 | tf_op jit(solution)/shard_map/agbp,bipc->agic/dot_general | solution.py:76
  388.6 22.0 %multiply_subtract_fusion.1 = (f32[1,512,32,256]{3,1,2,0:T(8,128)}, f32[1,512,32,256]{3,1,2,0:T(8,128)}) fusion(f32[2,512,32,256]{3,1,2,0:T(8,128)} %convolution_bitcast_fusion.1, f32[512,256]{1,0:T(8,128)S(1)} %get-tuple-element.29, f32[512,256]{1,0:T(8,128)S(1)} %get-tuple-element.30), kind=kLoop, calls=%fused_computation.21 | loop fusion | flops 25165824 | bytes 68157440 | tf_op jit(solution)/shard_map/sub | solution.py:20
  410.6 22.8 %fusion.22 = f32[512,2,32,32]{0,3,1,2:T(8,128)} fusion(f32[1,32,2,256]{3,1,2,0:T(8,128)S(1)} %get-tuple-element.21, f32[1,32,2,256]{3,1,2,0:T(8,128)S(1)} %get-tuple-element.20, f32[1,512,32,256]{3,1,2,0:T(8,128)} %get-tuple-element.11, f32[1,512,32,256]{3,1,2,0:T(8,128)} %get-tuple-element.10), kind=kOutput, calls=%fused_computation.31 | convolution fusion | flops 3230695424 | bytes 37879808 | tf_op jit(solution)/shard_map/ajbc,bgic->gaij/dot_general | solution.py:76
  444.3 143.5 %reduce-scatter.4.cloned.1.call-done = f32[16,2048]{1,0:T(8,128)} async-done(((f32[512,2048]{1,0:T(8,128)}), f32[16,2048]{1,0:T(8,128)}) %reduce-scatter.4.cloned.1.call-update) | async-done | bytes 131088
  634.4 57.8 %all-gather.2.cloned.1.call-done = f32[512,2048]{1,0:T(8,128)} async-done(((f32[16,2048]{1,0:T(8,128)}), f32[512,2048]{1,0:T(8,128)}) %all-gather.2.cloned.1.call-update) | async-done | bytes 4194320 | tf_op jit(solution)/shard_map/all_gather | solution.py:130
  697.5 20.8 %convolution_bitcast_fusion = f32[2,512,32,256]{3,1,2,0:T(8,128)} fusion(f32[512,2,32,32]{0,3,2,1:T(8,128)} %bitcast.179, f32[1,32,2,256]{3,1,2,0:T(8,128)} %copy-done.2, f32[1,32,2,256]{3,1,2,0:T(8,128)S(1)} %get-tuple-element.20), kind=kOutput, calls=%fused_computation.6 | convolution fusion | flops 3221258240 | bytes 37879808 | tf_op jit(solution)/shard_map/ajbc,gaij->bgic/dot_general | solution.py:76
  718.3 17.2 %multiply_subtract_fusion = (f32[1,512,32,256]{3,1,2,0:T(8,128)S(1)}, f32[1,512,32,256]{3,1,2,0:T(8,128)}) fusion(f32[2,512,32,256]{3,1,2,0:T(8,128)} %convolution_bitcast_fusion, f32[512,256]{1,0:T(8,128)} %get-tuple-element.28, f32[512,256]{1,0:T(8,128)S(1)} %get-tuple-element.30), kind=kLoop, calls=%fused_computation.19 | loop fusion | flops 25165824 | bytes 68157440 | tf_op jit(solution)/shard_map/sub | solution.py:20
  735.5 32.3 %fusion.12 = f32[32,256,2,256]{3,1,2,0:T(8,128)} fusion(f32[1,512,32,256]{3,1,2,0:T(8,128)} %get-tuple-element.9, f32[1,512,32,256]{3,1,2,0:T(8,128)S(1)} %get-tuple-element.8, f32[1,512,2,256]{3,1,2,0:T(8,128)S(1)} %get-tuple-element.19, f32[1,512,2,256]{3,1,2,0:T(8,128)S(1)} %get-tuple-element.18), kind=kOutput, calls=%fused_computation.22 | convolution fusion | flops 25778716672 | bytes 52428800 | tf_op jit(solution)/shard_map/agbp,agic->bipc/dot_general | solution.py:76
  767.8 20.2 %copy.123 = f32[32,256,2,256]{1,0,3,2:T(8,128)} copy(f32[32,256,2,256]{3,1,2,0:T(8,128)} %fusion.12) | data formatting | bytes 33554432 | tf_op jit(solution)/shard_map/agbp,agic->bipc/dot_general | solution.py:76
  788.1 9.8 multiply_subtract_fusion.2
  797.9 13.8 %fusion.18 = f32[2,32,256,256]{3,1,2,0:T(8,128)} fusion(f32[1,32,256,256]{3,1,2,0:T(8,128)} %get-tuple-element.13, f32[1,32,256,256]{3,1,2,0:T(8,128)S(1)} %get-tuple-element.12, f32[1,32,2,32]{3,1,2,0:T(8,128)S(1)} %copy-done.8, f32[1,32,2,32]{3,1,2,0:T(8,128)S(1)} %copy-done.6), kind=kOutput, calls=%fused_computation.28 | convolution fusion | flops 1619005440 | bytes 33570816 | tf_op jit(solution)/shard_map/aibq,aipc->bqpc/dot_general | solution.py:76
  811.7 15.5 %copy.126 = f32[2,32,256,256]{3,2,1,0:T(8,128)S(1)} copy(f32[2,32,256,256]{3,1,2,0:T(8,128)} %fusion.18) | data formatting | bytes 33554432 | tf_op jit(solution)/shard_map/aibq,aipc->bqpc/dot_general | solution.py:76
  827.2 46.1 %copy.127 = f32[2,8192,256]{2,0,1:T(2,128)} copy(f32[2,8192,256]{2,1,0:T(8,128)S(1)} %bitcast.176) | data formatting | bytes 33554432 | tf_op jit(solution)/shard_map/reshape | solution.py:138
  880.9 182.4 %all-to-all-done.1 = f32[2,8192,256]{2,0,1:T(2,128)} async-done(((f32[2,8192,256]{2,0,1:T(2,128)}), f32[2,8192,256]{2,0,1:T(2,128)}, u32[]{:S(2)}, u32[]{:S(2)}) %all-to-all-start.1) | async-done | bytes 16777248 | tf_op jit(solution)/shard_map/all_to_all | solution.py:137
  1063.3 12.8 %copy.128 = f32[2,8192,256]{2,1,0:T(8,128)} copy(f32[2,8192,256]{2,0,1:T(2,128)} %all-to-all-done.1) | data formatting | bytes 33554432 | tf_op jit(solution)/shard_map/all_to_all | solution.py:137
  1076.2 16.4 %copy.129 = f32[2,2048,4,256]{1,3,2,0:T(8,128)} copy(f32[2,2048,4,256]{3,1,2,0:T(8,128)} %bitcast.177) | data formatting | bytes 33554432 | tf_op jit(solution)/shard_map/all_to_all | solution.py:137
  1092.6 18.0 %copy.130 = f32[2,2048,1024]{2,1,0:T(8,128)} copy(f32[2,2048,1024]{1,2,0:T(8,128)} %bitcast.178) | data formatting | bytes 33554432
  (93 shorter events, 83.9 us)
Async XLA Ops:
  32.4 7.2 copy-start.12
  32.4 7.2 copy-start.13
  32.5 233.1 %all-to-all-start = ((f32[2,2048,1024]{1,0,2:T(2,128)}), f32[2,2048,1024]{1,0,2:T(2,128)}, u32[]{:S(2)}, u32[]{:S(2)}) async-start(f32[2,2048,1024]{1,0,2:T(2,128)} %copy.94), calls=%async_computation | async-start | bytes 33554432 | tf_op jit(solution)/shard_map/all_to_all | solution.py:99
  39.6 548.3 %reduce-scatter.4.cloned.1.call-start = ((), (), s32[]{:S(2)}) async-start(), calls=%async_computation.4 | async-start | bytes 4325376
  258.6 41.1 %copy-start.5 = (f32[1,32,2,32]{3,1,2,0:T(8,128)}, f32[1,32,2,32]{3,1,2,0:T(8,128)S(1)}, u32[]{:S(2)}) copy-start(f32[1,32,2,32]{3,1,2,0:T(8,128)S(1)} %get-tuple-element.26) | copy-start | bytes 24580
  258.7 41.1 %copy-start.7 = (f32[1,32,2,32]{3,1,2,0:T(8,128)}, f32[1,32,2,32]{3,1,2,0:T(8,128)S(1)}, u32[]{:S(2)}) copy-start(f32[1,32,2,32]{3,1,2,0:T(8,128)S(1)} %get-tuple-element.27) | copy-start | bytes 24580
  258.8 151.8 %copy-start.2 = (f32[1,32,2,256]{3,1,2,0:T(8,128)}, f32[1,32,2,256]{3,1,2,0:T(8,128)S(1)}, u32[]{:S(2)}) copy-start(f32[1,32,2,256]{3,1,2,0:T(8,128)S(1)} %get-tuple-element.21) | copy-start | bytes 196612
  260.0 66.0 %copy-start = (f32[32,256]{0,1:T(8,128)}, f32[32,256]{0,1:T(8,128)S(1)}, u32[]{:S(2)}) copy-start(f32[32,256]{0,1:T(8,128)S(1)} %get-tuple-element.42) | copy-start | bytes 98308
  299.8 26.3 %copy-start.3 = (f32[32,256]{0,1:T(8,128)S(1)}, f32[32,256]{0,1:T(8,128)}, u32[]{:S(2)}) copy-start(f32[32,256]{0,1:T(8,128)} %get-tuple-element.41) | copy-start | bytes 98308
  433.4 10.8 copy-start.14
  433.4 10.9 copy-start.10
  433.4 176.4 %copy-start.9 = (f32[16,2,128]{2,1,0:T(2,128)S(1)}, f32[16,2,128]{2,1,0:T(2,128)}, u32[]{:S(2)}) copy-start(f32[16,2,128]{2,1,0:T(2,128)} %param.9) | copy-start | bytes 49156
  443.9 248.3 %all-gather.2.cloned.1.call-start = ((), (), s32[]{:S(2)}) async-start(), calls=%async_computation.3 | async-start | bytes 4325376 | tf_op jit(solution)/shard_map/all_gather | solution.py:130
  444.2 165.7 %copy-start.11 = (f32[32]{0:T(128)}, f32[32]{0:T(128)S(1)}, u32[]{:S(2)}) copy-start(f32[32]{0:T(128)S(1)} %fusion.207) | copy-start | bytes 388
  767.8 20.2 %copy-start.1 = (f32[32,256]{0,1:T(8,128)S(1)}, f32[32,256]{0,1:T(8,128)}, u32[]{:S(2)}) copy-start(f32[32,256]{0,1:T(8,128)} %copy-done) | copy-start | bytes 98308
  767.8 20.2 %copy-start.4 = (f32[32,256]{0,1:T(8,128)S(1)}, f32[32,256]{0,1:T(8,128)}, u32[]{:S(2)}) copy-start(f32[32,256]{0,1:T(8,128)} %fusion.135) | copy-start | bytes 98308
  788.1 9.8 copy-start.6
  788.1 9.8 copy-start.8
  873.3 190.0 %all-to-all-start.1 = ((f32[2,8192,256]{2,0,1:T(2,128)}), f32[2,8192,256]{2,0,1:T(2,128)}, u32[]{:S(2)}, u32[]{:S(2)}) async-start(f32[2,8192,256]{2,0,1:T(2,128)} %copy.127), calls=%async_computation.1 | async-start | bytes 33554432 | tf_op jit(solution)/shard_map/all_to_all | solution.py:137
Sparse Core Ops, SparseCore 0:
  444.0 143.7 reduce-scatter.3
  633.3 58.8 all-gather.1
where the time goes:
time: 1130 us; the launch traced here: 1120 us
  waiting for transfers between devices  384 us (34%)
  blocking collectives  219 us (19%)
  local copies, waits for them, and re-layouts  213 us (19%)
  matrix products  194 us (17%)
  other arithmetic  79.1 us (7%)
  between operations  14.9 us (1%)
  starting transfers between devices  14.4 us (1%)
    unnamed x1, blocking collectives  219 us
    all_to_all x1, waiting for transfers between devices, per_device(): lax.all_to_all(rows.reshape(2, extent, cols), 'slab', split_axis=1, conca...  182 us
    dot_general x6, matrix products, product_high(): return jnp.einsum(form, left, right, precision=lax.Precision.HIGH)  158 us
    unnamed x3, waiting for transfers between devices  144 us
    sub x4, other arithmetic, complex_mul(): left[0] * right[0] - left[1] * right[1]  62.7 us
    all_gather x1, waiting for transfers between devices, per_device(): lax.all_gather(contrib.reshape(sub_count, 2 * SUB * SUB), both, axis=0, t...  57.8 us
    unnamed x37, local copies, waits for them, and re-layouts  53.7 us
    reshape x1, local copies, waits for them, and re-layouts, per_device(): rows.reshape(2, extent, cols)  46.1 us
  transfers between devices with their start and end apart: 4, of which 3 were waited for; matrix products, arithmetic and copies ran while one was open for 1% of the time, Pallas kernels for 0%

commit v1 on v0

--- a/solution.py
+++ b/solution.py
@@ -134,8 +134,14 @@
     back = product_high("agbp,agic->bipc", real_form(pick_u), spread)
     back = twist(lift_fine(conj(fine)), back) / extent
     rows = product_high("aibq,aipc->bqpc", real_form(coarse), back)
-    residual_image = lax.all_to_all(
-        rows.reshape(2, extent, cols), "slab", split_axis=1, concat_axis=2, tiled=True
+    residual_image = jnp.concatenate(
+        lax.all_to_all(
+            jnp.stack(jnp.split(rows.reshape(2, extent, cols), lax.axis_size("slab"), axis=1)),
+            "slab",
+            0,
+            0,
+        ),
+        axis=2,
     )
     return (residual_image, residual_vis)
 

time: 1130 us -> 1080 us (0.956)
  local copies, waits for them, and re-layouts: 213 us -> 158 us
    reshape x1, local copies, waits for them, and re-layouts: 46.1 us -> 16.5 us  [per_device(): jnp.concatenate(lax.all_to_all(jnp.stack(jnp.split(rows.reshape(2, extent...]
    all_to_all x2 -> x0, local copies, waits for them, and re-layouts: 29.3 us -> none  [per_device(): lax.all_to_all(rows.reshape(2, extent, cols), 'slab', split_axis=1, conca...]
where the time goes in v1:
time: 1080 us; the launch traced here: 1070 us
  waiting for transfers between devices  385 us (36%)
  blocking collectives  219 us (20%)
  matrix products  194 us (18%)
  local copies, waits for them, and re-layouts  158 us (15%)
  other arithmetic  89.7 us (8%)
  between operations  14.9 us (1%)
  starting transfers between devices  14.4 us (1%)
    unnamed x1, blocking collectives  219 us
    all_to_all x1, waiting for transfers between devices, per_device(): lax.all_to_all(jnp.stack(jnp.split(rows.reshape(2, extent, cols), lax.axi...  182 us
    dot_general x6, matrix products, product_high(): return jnp.einsum(form, left, right, precision=lax.Precision.HIGH)  158 us
    unnamed x3, waiting for transfers between devices  144 us
    sub x4, other arithmetic, complex_mul(): left[0] * right[0] - left[1] * right[1]  62.6 us
    all_gather x1, waiting for transfers between devices, per_device(): lax.all_gather(contrib.reshape(sub_count, 2 * SUB * SUB), both, axis=0, t...  58.5 us
    unnamed x37, local copies, waits for them, and re-layouts  53.7 us
    dot_general x24, matrix products, complex_einsum(): jnp.einsum(form, first, second, precision=lax.Precision.HIGHEST)  36.2 us
  transfers between devices with their start and end apart: 4, of which 3 were waited for; matrix products, arithmetic and copies ran while one was open for 1% of the time, Pallas kernels for 0%

profile of v1, /device:TPU:0, one launch (start us, length us, event | category | flops | bytes accessed | tf_op | source)
XLA Modules:
  0.0 1075.0 jit_solution(18249855540050834867)
XLA Ops:
  7.2 25.3 %copy.97 = f32[2,2048,1024]{1,0,2:T(2,128)} copy(f32[2,2048,1024]{2,1,0:T(8,128)} %param.7) | data formatting | bytes 33554432 | tf_op args[0]
  32.5 7.1 all-to-all-start
  39.8 218.7 %all-reduce = s32[512]{0:T(512)S(1)} all-reduce(s32[512]{0:T(512)S(1)} %fusion.206), channel_id=1, replica_groups=mesh['slab'=4,'bl'=8] {'slab','bl'}, use_global_device_ids=true, to_apply=%add | all-reduce | flops 512 | bytes 4096
  265.5 17.7 %copy.98 = f32[2,2048,1024]{1,2,0:T(8,128)} copy(f32[2,2048,1024]{1,0,2:T(2,128)} %all-to-all-done) | data formatting | bytes 33554432 | tf_op jit(solution)/shard_map/all_to_all | solution.py:99
  283.3 16.5 %copy.99 = f32[2,4,2048,256]{3,2,1,0:T(8,128)} copy(f32[2,4,2048,256]{2,3,1,0:T(8,128)} %bitcast.182) | data formatting | bytes 33554432 | tf_op jit(solution)/shard_map/all_to_all | solution.py:99
  299.8 26.3 %fusion.15 = f32[2,32,256,256]{3,1,2,0:T(8,128)} fusion(f32[2,32,256,256]{3,2,1,0:T(8,128)} %bitcast.181, f32[1,32,2,32]{3,1,2,0:T(8,128)S(1)} %get-tuple-element.31, f32[1,32,2,32]{3,1,2,0:T(8,128)S(1)} %get-tuple-element.30), kind=kOutput, calls=%fused_computation.28 | convolution fusion | flops 1610616832 | bytes 33570816 | tf_op jit(solution)/shard_map/aibq,bqpc->aipc/dot_general | solution.py:76
  326.1 13.7 %multiply_subtract_fusion.3 = (f32[1,32,256,256]{3,1,2,0:T(8,128)}, f32[1,32,256,256]{3,1,2,0:T(8,128)}) fusion(f32[2,32,256,256]{3,1,2,0:T(8,128)} %fusion.15, f32[32,256]{0,1:T(8,128)S(1)} %copy-done.3, f32[32,256]{0,1:T(8,128)S(1)} %get-tuple-element.46), kind=kLoop, calls=%fused_computation.27 | loop fusion | flops 12582912 | bytes 33619968 | tf_op jit(solution)/shard_map/sub | solution.py:20
  346.4 42.3 %convolution_bitcast_fusion.1 = f32[2,512,32,256]{3,1,2,0:T(8,128)} fusion(f32[2,32,256,256]{3,1,2,0:T(8,128)S(1)} %pad_maximum_fusion, f32[1,512,2,256]{3,1,2,0:T(8,128)S(1)} %get-tuple-element.23, f32[1,512,2,256]{3,1,2,0:T(8,128)S(1)} %get-tuple-element.22), kind=kOutput, calls=%fused_computation.7 | convolution fusion | flops 25770328064 | bytes 52428800 | tf_op jit(solution)/shard_map/agbp,bipc->agic/dot_general | solution.py:76
  388.7 21.9 %multiply_subtract_fusion.1 = (f32[1,512,32,256]{3,1,2,0:T(8,128)}, f32[1,512,32,256]{3,1,2,0:T(8,128)}) fusion(f32[2,512,32,256]{3,1,2,0:T(8,128)} %convolution_bitcast_fusion.1, f32[512,256]{1,0:T(8,128)S(1)} %get-tuple-element.33, f32[512,256]{1,0:T(8,128)S(1)} %get-tuple-element.34), kind=kLoop, calls=%fused_computation.22 | loop fusion | flops 25165824 | bytes 68157440 | tf_op jit(solution)/shard_map/sub | solution.py:20
  410.6 22.8 %fusion.22 = f32[512,2,32,32]{0,3,1,2:T(8,128)} fusion(f32[1,32,2,256]{3,1,2,0:T(8,128)S(1)} %get-tuple-element.25, f32[1,32,2,256]{3,1,2,0:T(8,128)S(1)} %get-tuple-element.24, f32[1,512,32,256]{3,1,2,0:T(8,128)} %get-tuple-element.11, f32[1,512,32,256]{3,1,2,0:T(8,128)} %get-tuple-element.10), kind=kOutput, calls=%fused_computation.36 | convolution fusion | flops 3230695424 | bytes 37879808 | tf_op jit(solution)/shard_map/ajbc,bgic->gaij/dot_general | solution.py:76
  444.3 143.6 %reduce-scatter.4.cloned.1.call-done = f32[16,2048]{1,0:T(8,128)} async-done(((f32[512,2048]{1,0:T(8,128)}), f32[16,2048]{1,0:T(8,128)}) %reduce-scatter.4.cloned.1.call-update) | async-done | bytes 131088
  634.4 58.5 %all-gather.2.cloned.1.call-done = f32[512,2048]{1,0:T(8,128)} async-done(((f32[16,2048]{1,0:T(8,128)}), f32[512,2048]{1,0:T(8,128)}) %all-gather.2.cloned.1.call-update) | async-done | bytes 4194320 | tf_op jit(solution)/shard_map/all_gather | solution.py:130
  698.2 20.8 %convolution_bitcast_fusion = f32[2,512,32,256]{3,1,2,0:T(8,128)} fusion(f32[512,2,32,32]{0,3,2,1:T(8,128)} %bitcast.184, f32[1,32,2,256]{3,1,2,0:T(8,128)} %copy-done.2, f32[1,32,2,256]{3,1,2,0:T(8,128)S(1)} %get-tuple-element.24), kind=kOutput, calls=%fused_computation.6 | convolution fusion | flops 3221258240 | bytes 37879808 | tf_op jit(solution)/shard_map/ajbc,gaij->bgic/dot_general | solution.py:76
  719.0 17.2 %multiply_subtract_fusion = (f32[1,512,32,256]{3,1,2,0:T(8,128)S(1)}, f32[1,512,32,256]{3,1,2,0:T(8,128)}) fusion(f32[2,512,32,256]{3,1,2,0:T(8,128)} %convolution_bitcast_fusion, f32[512,256]{1,0:T(8,128)} %get-tuple-element.32, f32[512,256]{1,0:T(8,128)S(1)} %get-tuple-element.34), kind=kLoop, calls=%fused_computation.20 | loop fusion | flops 25165824 | bytes 68157440 | tf_op jit(solution)/shard_map/sub | solution.py:20
  736.2 32.2 %fusion.12 = f32[32,256,2,256]{3,1,2,0:T(8,128)} fusion(f32[1,512,32,256]{3,1,2,0:T(8,128)} %get-tuple-element.9, f32[1,512,32,256]{3,1,2,0:T(8,128)S(1)} %get-tuple-element.8, f32[1,512,2,256]{3,1,2,0:T(8,128)S(1)} %get-tuple-element.23, f32[1,512,2,256]{3,1,2,0:T(8,128)S(1)} %get-tuple-element.22), kind=kOutput, calls=%fused_computation.23 | convolution fusion | flops 25778716672 | bytes 52428800 | tf_op jit(solution)/shard_map/agbp,agic->bipc/dot_general | solution.py:76
  768.4 20.2 %copy.126 = f32[32,256,2,256]{1,0,3,2:T(8,128)} copy(f32[32,256,2,256]{3,1,2,0:T(8,128)} %fusion.12) | data formatting | bytes 33554432 | tf_op jit(solution)/shard_map/agbp,agic->bipc/dot_general | solution.py:76
  788.7 9.8 multiply_subtract_fusion.2
  798.5 13.8 %fusion.18 = f32[2,32,256,256]{3,1,2,0:T(8,128)} fusion(f32[1,32,256,256]{3,1,2,0:T(8,128)} %get-tuple-element.13, f32[1,32,256,256]{3,1,2,0:T(8,128)S(1)} %get-tuple-element.12, f32[1,32,2,32]{3,1,2,0:T(8,128)S(1)} %copy-done.8, f32[1,32,2,32]{3,1,2,0:T(8,128)S(1)} %copy-done.6), kind=kOutput, calls=%fused_computation.29 | convolution fusion | flops 1619005440 | bytes 33570816 | tf_op jit(solution)/shard_map/aibq,aipc->bqpc/dot_general | solution.py:76
  812.3 15.5 %copy.129 = f32[2,32,256,256]{3,2,1,0:T(8,128)S(1)} copy(f32[2,32,256,256]{3,1,2,0:T(8,128)} %fusion.18) | data formatting | bytes 33554432 | tf_op jit(solution)/shard_map/aibq,aipc->bqpc/dot_general | solution.py:76
  832.5 10.7 pad_maximum_fusion.1
  843.2 7.0 all-to-all-start.1
  850.8 182.4 %all-to-all-done.1 = f32[4,2,2048,256]{3,2,1,0:T(8,128)} async-done(((f32[4,2,2048,256]{3,2,1,0:T(8,128)}), f32[4,2,2048,256]{3,2,1,0:T(8,128)}, u32[]{:S(2)}, u32[]{:S(2)}) %all-to-all-start.1) | async-done | bytes 16777248 | tf_op jit(solution)/shard_map/all_to_all | solution.py:138
  1033.2 16.5 %copy.130 = f32[2,2048,4,256]{1,3,2,0:T(8,128)} copy(f32[2,2048,4,256]{3,1,0,2:T(8,128)} %bitcast.64) | data formatting | bytes 33554432 | tf_op jit(solution)/shard_map/reshape | solution.py:137
  1049.7 18.0 %copy.131 = f32[2,2048,1024]{2,1,0:T(8,128)} copy(f32[2,2048,1024]{1,2,0:T(8,128)} %bitcast.183) | data formatting | bytes 33554432
  (93 shorter events, 81.5 us)
Async XLA Ops:
  32.4 7.2 copy-start.12
  32.4 7.2 copy-start.13
  32.5 233.1 %all-to-all-start = ((f32[2,2048,1024]{1,0,2:T(2,128)}), f32[2,2048,1024]{1,0,2:T(2,128)}, u32[]{:S(2)}, u32[]{:S(2)}) async-start(f32[2,2048,1024]{1,0,2:T(2,128)} %copy.97), calls=%async_computation | async-start | bytes 33554432 | tf_op jit(solution)/shard_map/all_to_all | solution.py:99
  39.6 548.3 %reduce-scatter.4.cloned.1.call-start = ((), (), s32[]{:S(2)}) async-start(), calls=%async_computation.4 | async-start | bytes 4325376
  258.7 41.1 %copy-start.5 = (f32[1,32,2,32]{3,1,2,0:T(8,128)}, f32[1,32,2,32]{3,1,2,0:T(8,128)S(1)}, u32[]{:S(2)}) copy-start(f32[1,32,2,32]{3,1,2,0:T(8,128)S(1)} %get-tuple-element.30) | copy-start | bytes 24580
  258.7 41.1 %copy-start.7 = (f32[1,32,2,32]{3,1,2,0:T(8,128)}, f32[1,32,2,32]{3,1,2,0:T(8,128)S(1)}, u32[]{:S(2)}) copy-start(f32[1,32,2,32]{3,1,2,0:T(8,128)S(1)} %get-tuple-element.31) | copy-start | bytes 24580
  258.9 151.7 %copy-start.2 = (f32[1,32,2,256]{3,1,2,0:T(8,128)}, f32[1,32,2,256]{3,1,2,0:T(8,128)S(1)}, u32[]{:S(2)}) copy-start(f32[1,32,2,256]{3,1,2,0:T(8,128)S(1)} %get-tuple-element.25) | copy-start | bytes 196612
  260.1 66.0 %copy-start = (f32[32,256]{0,1:T(8,128)}, f32[32,256]{0,1:T(8,128)S(1)}, u32[]{:S(2)}) copy-start(f32[32,256]{0,1:T(8,128)S(1)} %get-tuple-element.46) | copy-start | bytes 98308
  299.8 26.3 %copy-start.3 = (f32[32,256]{0,1:T(8,128)S(1)}, f32[32,256]{0,1:T(8,128)}, u32[]{:S(2)}) copy-start(f32[32,256]{0,1:T(8,128)} %get-tuple-element.45) | copy-start | bytes 98308
  433.4 10.8 %copy-start.14 = (s32[16]{0:T(128)S(1)}, s32[16]{0:T(128)}, u32[]{:S(2)}) copy-start(s32[16]{0:T(128)} %param.12) | copy-start | bytes 196
  433.4 10.9 %copy-start.10 = (f32[16,2,128]{2,1,0:T(2,128)S(1)}, f32[16,2,128]{2,1,0:T(2,128)}, u32[]{:S(2)}) copy-start(f32[16,2,128]{2,1,0:T(2,128)} %param.8) | copy-start | bytes 49156
  433.4 176.5 %copy-start.9 = (f32[16,2,128]{2,1,0:T(2,128)S(1)}, f32[16,2,128]{2,1,0:T(2,128)}, u32[]{:S(2)}) copy-start(f32[16,2,128]{2,1,0:T(2,128)} %param.9) | copy-start | bytes 49156
  443.8 249.0 %all-gather.2.cloned.1.call-start = ((), (), s32[]{:S(2)}) async-start(), calls=%async_computation.3 | async-start | bytes 4325376 | tf_op jit(solution)/shard_map/all_gather | solution.py:130
  444.1 165.7 %copy-start.11 = (f32[32]{0:T(128)}, f32[32]{0:T(128)S(1)}, u32[]{:S(2)}) copy-start(f32[32]{0:T(128)S(1)} %fusion.207) | copy-start | bytes 388
  768.4 20.2 %copy-start.1 = (f32[32,256]{0,1:T(8,128)S(1)}, f32[32,256]{0,1:T(8,128)}, u32[]{:S(2)}) copy-start(f32[32,256]{0,1:T(8,128)} %copy-done) | copy-start | bytes 98308
  768.4 20.2 %copy-start.4 = (f32[32,256]{0,1:T(8,128)S(1)}, f32[32,256]{0,1:T(8,128)}, u32[]{:S(2)}) copy-start(f32[32,256]{0,1:T(8,128)} %fusion.135) | copy-start | bytes 98308
  788.6 9.8 copy-start.6
  788.6 9.8 copy-start.8
  843.2 190.0 %all-to-all-start.1 = ((f32[4,2,2048,256]{3,2,1,0:T(8,128)}), f32[4,2,2048,256]{3,2,1,0:T(8,128)}, u32[]{:S(2)}, u32[]{:S(2)}) async-start(f32[4,2,2048,256]{3,2,1,0:T(8,128)} %pad_maximum_fusion.1), calls=%async_computation.1 | async-start | bytes 33554432 | tf_op jit(solution)/shard_map/all_to_all | solution.py:138
Sparse Core Ops, SparseCore 0:
  444.0 143.8 reduce-scatter.3
  633.4 59.4 all-gather.1
